TPU v7x, 32 devices: a whole 2x2x4 slice. The times are simulated.
32 devices in a mesh: ctx: 16 (over z, x, core), exp: 2 (over y).
Axes of the slice: x: 2, y: 2, z: 4, core: 2. Of those that a mesh axis runs over, the one named last changes fastest.
Arguments:
- resid: bfloat16 [2048, 2880], P(('ctx', 'exp')), may hold values from -3 to 3
- queries: bfloat16 [2048, 2048], P('ctx', 'exp'), may hold values from -8 to 8
- keys: bfloat16 [2048, 256], P('ctx'), may hold values from -8 to 8
- values: bfloat16 [2048, 256], P('ctx'), may hold values from -6 to 6
- sinks: float32 [32], P('exp'), may hold values from 0 to 6
- out_weight: bfloat16 [2048, 2880], P('exp'), may hold values from -0.125 to 0.125
- norm_gain: float32 [2880], replicated, may hold values from 0.5 to 1.5
- gate_weight: bfloat16 [16, 2880, 1536], P('ctx', None, 'exp'), may hold values from -0.109375 to 0.109375
- up_weight: bfloat16 [16, 2880, 1536], P('ctx', None, 'exp'), may hold values from -0.109375 to 0.109375
- down_weight: bfloat16 [16, 1536, 2880], P('ctx', 'exp'), may hold values from -0.15625 to 0.15625
- routes: int32 [2048, 4], P('ctx'), may hold values from 0 to 15, all different within a row; in each aligned block of 128 rows (0 to 127, 128 to 255, ...) at most 64 rows name the same one
- route_weights: float32 [2048, 4], P('ctx'), may hold values from 0.05 to 0.6
Outputs:
- block_out: bfloat16 [2048, 2880], P(('ctx', 'exp'))
Inputs may be any that keep to these rules, and one draw needn't show every extreme that they name: `routes`: in each aligned block of 128 rows no expert is named by more than 64 rows, a bound that some block reaches; a row names 4 different experts.
All inputs are finite; a program needn't handle non-finite values.
Results may differ from a plain program's by a relative error of at most 0.0085.
Values may be sent and summed in bfloat16 or wider, within the bound.
A program may use at most 128 MiB of HBM per device.

v0:
```python
import jax
import jax.numpy as jnp
from jax import lax
from jax.sharding import PartitionSpec as P

HD = 64
QH = 32
KVH = 4
TOP = 4
WIN = 128
NEG_FILL = -1e30
EPSILON = 1e-05


def shifted(array, axis, by):
    size = lax.axis_size(axis)
    pairs = [(i, i + by) for i in range(size) if 0 <= i + by < size]
    return lax.ppermute(array, axis, pairs)


def per_device(
    resid,
    queries,
    keys,
    values,
    sinks,
    out_weight,
    norm_gain,
    gate_weight,
    up_weight,
    down_weight,
    routes,
    route_weights,
):
    rows_here = queries.shape[0]
    local_heads = queries.shape[1] // HD
    per_group = QH // KVH
    kv_count = max(1, local_heads // per_group)
    head_reps = local_heads // kv_count
    exp_rank = lax.axis_index("exp")
    ctx_rank = lax.axis_index("ctx")
    kv_first = exp_rank * local_heads // per_group
    prior_keys, prior_values = shifted((keys, values), "ctx", 1)
    keys_ext = jnp.concatenate([prior_keys, keys], 0).reshape(rows_here + WIN, KVH, HD)
    values_ext = jnp.concatenate([prior_values, values], 0).reshape(rows_here + WIN, KVH, HD)
    keys_sel = lax.dynamic_slice_in_dim(keys_ext, kv_first, kv_count, 1)
    values_sel = lax.dynamic_slice_in_dim(values_ext, kv_first, kv_count, 1)
    query_four = queries.reshape(rows_here, kv_count, head_reps, HD)
    scores = jnp.einsum(
        "qgrd,kgd->grqk", query_four, keys_sel, preferred_element_type=jnp.float32
    ) * HD ** (-0.5)
    first_pos = ctx_rank * rows_here
    query_pos = first_pos + jnp.arange(rows_here, dtype=jnp.int32)
    key_pos = first_pos - WIN + jnp.arange(rows_here + WIN, dtype=jnp.int32)
    visible = (
        (key_pos[None, :] <= query_pos[:, None])
        & (key_pos[None, :] > query_pos[:, None] - WIN)
        & (key_pos[None, :] >= 0)
    )
    masked = jnp.where(visible[None, None], scores, NEG_FILL)
    sink_cols = sinks.reshape(kv_count, head_reps)[:, :, None]
    row_max = jnp.maximum(jnp.max(masked, axis=-1), sink_cols)
    exp_terms = jnp.where(visible[None, None], jnp.exp(masked - row_max[..., None]), 0.0)
    denominator = jnp.sum(exp_terms, axis=-1) + jnp.exp(sink_cols - row_max)
    soft_weights = (exp_terms / denominator[..., None]).astype(jnp.bfloat16)
    attended = jnp.einsum(
        "grqk,kgd->qgrd", soft_weights, values_sel, preferred_element_type=jnp.float32
    )
    attended = attended.reshape(rows_here, local_heads * HD).astype(jnp.bfloat16)
    projected = lax.psum_scatter(
        jnp.dot(attended, out_weight, preferred_element_type=jnp.float32),
        "exp",
        scatter_dimension=0,
        tiled=True,
    )
    after_attention = resid.astype(jnp.float32) + projected
    mean_square = jnp.mean(after_attention * after_attention, axis=-1, keepdims=True)
    normed = (after_attention * lax.rsqrt(mean_square + EPSILON) * norm_gain).astype(jnp.bfloat16)
    all_normed = lax.all_gather(normed, "exp", axis=0, tiled=True)
    n_experts = lax.axis_size("ctx")
    capacity = 2 * rows_here * TOP // n_experts
    width = all_normed.shape[1]
    flat_ids = routes.reshape(-1)
    one_hot = (flat_ids[:, None] == jnp.arange(n_experts, dtype=jnp.int32)[None, :]).astype(
        jnp.int32
    )
    rank_in = jnp.sum(jnp.cumsum(one_hot, axis=0) * one_hot, axis=1) - 1
    slot_index = flat_ids * capacity + rank_in
    token_of = jnp.arange(rows_here * TOP, dtype=jnp.int32) // TOP
    outgoing = (
        jnp.zeros((n_experts * capacity, width), jnp.bfloat16)
        .at[slot_index]
        .set(all_normed[token_of])
    )
    outgoing = outgoing.reshape(n_experts, capacity, width)
    gate_local = gate_weight[0]
    up_local = up_weight[0]
    down_local = down_weight[0]
    slot_block = lax.all_to_all(outgoing, "ctx", split_axis=0, concat_axis=0, tiled=True)
    block_shape = slot_block.shape
    flat_rows = slot_block.reshape(-1, block_shape[2])
    gate_val = jnp.dot(flat_rows, gate_local, preferred_element_type=jnp.float32)
    up_val = jnp.dot(flat_rows, up_local, preferred_element_type=jnp.float32)
    activated = (jax.nn.silu(gate_val) * up_val).astype(jnp.bfloat16)
    partial_rows = jnp.dot(activated, down_local, preferred_element_type=jnp.float32).astype(
        jnp.bfloat16
    )
    partial_out = partial_rows.reshape(block_shape)
    returned = lax.all_to_all(partial_out, "ctx", split_axis=0, concat_axis=0, tiled=True)
    flat_back = returned.reshape(n_experts * capacity, width)
    picked = flat_back[slot_index].reshape(rows_here, TOP, width)
    combined = jnp.sum(picked.astype(jnp.float32) * route_weights[:, :, None], axis=1)
    expert_mix = lax.psum_scatter(
        combined.astype(jnp.bfloat16), "exp", scatter_dimension=0, tiled=True
    ).astype(jnp.float32)
    return (after_attention + expert_mix).astype(jnp.bfloat16)


def solution(mesh):
    in_specs = (
        P(("ctx", "exp"), None),
        P("ctx", "exp"),
        P("ctx", None),
        P("ctx", None),
        P("exp"),
        P("exp", None),
        P(),
        P("ctx", None, "exp"),
        P("ctx", None, "exp"),
        P("ctx", "exp", None),
        P("ctx", None),
        P("ctx", None),
    )
    out_specs = P(("ctx", "exp"), None)
    return jax.shard_map(
        per_device, mesh=mesh, in_specs=in_specs, out_specs=out_specs, check_vma=False
    )
```

profile of v0, /device:TPU:0, one launch (start us, length us, event | category | flops | bytes accessed | tf_op | source)
XLA Modules:
  0.0 440.2 jit_solution(13573109594631216473)
XLA Ops:
  6.5 2.5 collective-permute-start.1
  9.1 4.5 %collective-permute-start = (bf16[128,256]{1,0:T(8,128)(2,1)}, bf16[128,256]{1,0:T(8,128)(2,1)S(1)}, u32[]{:S(2)}, u32[]{:S(2)}) collective-permute-start(bf16[128,256]{1,0:T(8,128)(2,1)} %param.15), channel_id=1, source_target_pairs={{0,2},{2,4},{4,6},{6,8},{8,10},{10,12},{12,14},{14,16},{16,18},{18... | collective-permute-start | bytes 196616 | tf_op jit(solution)/shard_map/ppermute | solution.py:18
  13.8 1.1 copy.21
  14.9 0.7 max.17
  15.6 0.8 pad_maximum_fusion.1
  18.6 6.0 %fusion.29 = f32[128,2880]{1,0:T(8,128)} fusion(bf16[128,1024]{0,1:T(8,128)(2,1)S(1)} %bitcast.75, bf16[1024,2880]{0,1:T(8,128)(2,1)} %param.17), kind=kOutput, calls=%fused_computation.64 | convolution fusion | flops 754974720 | bytes 7634944 | tf_op jit(solution)/shard_map/dot_general | solution.py:71
  25.0 1.2 reduce-window.6
  26.8 23.8 %reduce-scatter.3.cloned.1.call-done = f32[64,2880]{1,0:T(8,128)} async-done(((f32[128,2880]{1,0:T(8,128)}), f32[64,2880]{1,0:T(8,128)}) %reduce-scatter.3.cloned.1.call-update) | async-done | bytes 737296 | tf_op jit(solution)/shard_map/reduce_scatter | solution.py:70
  50.5 1.3 multiply_reduce_fusion.1
  51.9 1.3 multiply_convert_fusion.1
  53.2 11.3 %all_gather.3 = bf16[128,2880]{1,0:T(8,128)(2,1)S(1)} all-gather(bf16[64,2880]{1,0:T(8,128)(2,1)S(1)} %multiply_convert_fusion.1), channel_id=1, replica_groups=mesh['ctx'=16,'exp'=2] {'exp'}, dimensions={0}, use_global_device_ids=true | all-gather | bytes 1105920 | tf_op jit(solution)/shard_map/all_gather | solution.py:79
  64.5 17.9 %scatter_custom_fusion = bf16[1024,2880]{1,0:T(8,128)(2,1)} fusion(s32[512]{0:T(512)S(1)} %bitcast.77, bf16[128,2880]{1,0:T(8,128)(2,1)S(1)} %all_gather.3, s32[1024]{0:T(1024)S(1)} %pad_clamp_fusion.1, bf16[]{:T(256)} %constant.72.clone.1), kind=kCustom, calls=%fused_computation.11 | custom fusion | bytes 5898242 | tf_op jit(solution)/shard_map/scatter | solution.py:93
  82.4 138.2 %all_to_all.10 = bf16[16,64,2880]{2,1,0:T(8,128)(2,1)S(1)} all-to-all(bf16[16,64,2880]{2,1,0:T(8,128)(2,1)} %bitcast.70), channel_id=1, replica_groups=mesh['ctx'=16,'exp'=2] {'ctx'}, dimensions={0} | all-to-all | bytes 11796480 | tf_op jit(solution)/shard_map/all_to_all | solution.py:99
  220.6 2.6 copy-done.1
  223.2 9.0 %fusion.1 = f32[1024,768]{1,0:T(8,128)} fusion(bf16[1024,2880]{1,0:T(8,128)(2,1)S(1)} %bitcast.71, bf16[1,2880,768]{2,1,0:T(8,128)(2,1)} %param.20), kind=kOutput, calls=%fused_computation.6 | convolution fusion | flops 4529848320 | bytes 13467648 | tf_op jit(solution)/shard_map/dot_general | solution.py:103
  232.2 16.5 %convolution_convert_fusion = bf16[1024,2880]{0,1:T(8,128)(2,1)} fusion(bf16[1,768,2880]{1,2,0:T(8,128)(2,1)} %param.21, f32[1024,768]{1,0:T(8,128)} %fusion.1, bf16[1024,2880]{1,0:T(8,128)(2,1)} %bitcast.72, bf16[1,2880,768]{2,1,0:T(8,128)(2,1)} %param.19), kind=kOutput, calls=%fused_computation.4 | convolution fusion | flops 9067364352 | bytes 23789568 | tf_op jit(solution)/shard_map/dot_general | solution.py:105
  248.8 8.5 %copy.27 = bf16[1024,2880]{1,0:T(8,128)(2,1)} copy(bf16[1024,2880]{0,1:T(8,128)(2,1)} %convolution_convert_fusion) | data formatting | bytes 11796480 | tf_op jit(solution)/shard_map/convert_element_type | solution.py:105
  257.3 4.8 %all-to-all-start.1 = ((bf16[16,64,2880]{2,1,0:T(8,128)(2,1)}), bf16[16,64,2880]{2,1,0:T(8,128)(2,1)}, u32[]{:S(2)}, u32[]{:S(2)}) async-start(bf16[16,64,2880]{2,1,0:T(8,128)(2,1)} %bitcast.69), calls=%async_computation.2 | async-start | bytes 12058624 | tf_op jit(solution)/shard_map/all_to_all | solution.py:109
  262.2 109.3 %all-to-all-done.1 = bf16[16,64,2880]{2,1,0:T(8,128)(2,1)} async-done(((bf16[16,64,2880]{2,1,0:T(8,128)(2,1)}), bf16[16,64,2880]{2,1,0:T(8,128)(2,1)}, u32[]{:S(2)}, u32[]{:S(2)}) %all-to-all-start.1) | async-done | bytes 5898272 | tf_op jit(solution)/shard_map/all_to_all | solution.py:109
  371.5 9.5 %gather_fusion = bf16[512,2880]{1,0:T(8,128)(2,1)S(1)} fusion(bf16[1024,2880]{1,0:T(8,128)(2,1)} %bitcast.20, s32[1024]{0:T(1024)S(1)} %pad_clamp_fusion), kind=kCustom, calls=%fused_computation.1 | custom fusion | bytes 5900288 | tf_op jit(solution)/shard_map/gather | solution.py:111
  381.0 3.6 reshape.235
  384.6 8.0 %multiply_reduce_fusion = bf16[128,2880]{1,0:T(8,128)(2,1)} fusion(f32[128,4,2880]{2,1,0:T(4,128)} %reshape.235, f32[128,4]{1,0:T(8,128)S(1)} %copy.28), kind=kLoop, calls=%fused_computation.3 | loop fusion | flops 2580480 | bytes 6637568 | tf_op jit(solution)/shard_map/reduce_sum | solution.py:112
  392.6 38.7 %reduce-scatter.5.cloned.1.call-done = bf16[64,2880]{1,0:T(8,128)(2,1)} async-done(((bf16[128,2880]{1,0:T(8,128)(2,1)}), bf16[64,2880]{1,0:T(8,128)(2,1)}) %reduce-scatter.5.cloned.1.call-update) | async-done | bytes 368656 | tf_op jit(solution)/shard_map/reduce_scatter | solution.py:113
  431.3 1.8 add_convert_fusion
  (49 shorter events, 3.4 us)
Async XLA Ops:
  6.5 11.2 %copy-start.3 = (bf16[128,256]{1,0:T(8,128)(2,1)S(1)}, bf16[128,256]{1,0:T(8,128)(2,1)}, u32[]{:S(2)}) copy-start(bf16[128,256]{1,0:T(8,128)(2,1)} %param.15) | copy-start | bytes 196612
  6.5 44.0 %reduce-scatter.3.cloned.1.call-start = ((), (), s32[]{:S(2)}) async-start(), calls=%async_computation.4 | async-start | bytes 2260992 | tf_op jit(solution)/shard_map/reduce_scatter | solution.py:70
  6.5 9.1 %collective-permute-start.1 = (bf16[128,256]{1,0:T(8,128)(2,1)}, bf16[128,256]{1,0:T(8,128)(2,1)S(1)}, u32[]{:S(2)}, u32[]{:S(2)}) collective-permute-start(bf16[128,256]{1,0:T(8,128)(2,1)} %param.14), channel_id=1, source_target_pairs={{0,2},{2,4},{4,6},{6,8},{8,10},{10,12},{12,14},{14,16},{16,18},{18... | collective-permute-start | bytes 196616 | tf_op jit(solution)/shard_map/ppermute | solution.py:18
  9.1 8.7 %collective-permute-start = (bf16[128,256]{1,0:T(8,128)(2,1)}, bf16[128,256]{1,0:T(8,128)(2,1)S(1)}, u32[]{:S(2)}, u32[]{:S(2)}) collective-permute-start(bf16[128,256]{1,0:T(8,128)(2,1)} %param.15), channel_id=1, source_target_pairs={{0,2},{2,4},{4,6},{6,8},{8,10},{10,12},{12,14},{14,16},{16,18},{18... | collective-permute-start | bytes 196616 | tf_op jit(solution)/shard_map/ppermute | solution.py:18
  18.6 6.0 %copy-start.5 = (s32[128,4]{0,1:T(4,128)S(1)}, s32[128,4]{0,1:T(4,128)}, u32[]{:S(2)}) copy-start(s32[128,4]{0,1:T(4,128)} %param.22) | copy-start | bytes 6148
  18.6 31.9 %copy-start.2 = (bf16[64,2880]{1,0:T(8,128)(2,1)S(1)}, bf16[64,2880]{1,0:T(8,128)(2,1)}, u32[]{:S(2)}) copy-start(bf16[64,2880]{1,0:T(8,128)(2,1)} %param.12) | copy-start | bytes 1105924
  24.6 27.3 %copy-start.4 = (f32[2880]{0:T(1024)S(1)}, f32[2880]{0:T(1024)}, u32[]{:S(2)}) copy-start(f32[2880]{0:T(1024)} %param.18) | copy-start | bytes 34564
  220.6 2.6 copy-start.1
  257.3 4.8 %copy-start.6 = (f32[128,4]{0,1:T(4,128)S(1)}, f32[128,4]{0,1:T(4,128)}, u32[]{:S(2)}) copy-start(f32[128,4]{0,1:T(4,128)} %param.23) | copy-start | bytes 6148
  257.3 114.2 %all-to-all-start.1 = ((bf16[16,64,2880]{2,1,0:T(8,128)(2,1)}), bf16[16,64,2880]{2,1,0:T(8,128)(2,1)}, u32[]{:S(2)}, u32[]{:S(2)}) async-start(bf16[16,64,2880]{2,1,0:T(8,128)(2,1)} %bitcast.69), calls=%async_computation.2 | async-start | bytes 12058624 | tf_op jit(solution)/shard_map/all_to_all | solution.py:109
  262.0 169.3 %reduce-scatter.5.cloned.1.call-start = ((), (), s32[]{:S(2)}) async-start(), calls=%async_computation.5 | async-start | bytes 1130496 | tf_op jit(solution)/shard_map/reduce_scatter | solution.py:113
  384.6 46.8 %copy-start = (f32[64,2880]{1,0:T(8,128)S(1)}, f32[64,2880]{1,0:T(8,128)}, u32[]{:S(2)}) copy-start(f32[64,2880]{1,0:T(8,128)} %reduce-scatter.3.cloned.1.call-done) | copy-start | bytes 2211844
Sparse Core Ops, SparseCore 0:
  24.8 25.7 reduce-scatter.2
  392.7 38.5 reduce-scatter.4
where the time goes:
time: 445 us; the launch traced here: 440 us
  waiting for transfers between devices  172 us (39%)
  blocking collectives  150 us (34%)
  local copies, waits for them, and re-layouts  45 us (10%)
  matrix products  32.8 us (7%)
  other arithmetic  15.4 us (3%)
  between operations  13.9 us (3%)
  starting transfers between devices  11.8 us (3%)
    all_to_all x1, blocking collectives, per_device(): lax.all_to_all(outgoing, 'ctx', split_axis=0, concat_axis=0, tiled=True)  138 us
    all_to_all x1, waiting for transfers between devices, per_device(): lax.all_to_all(partial_out, 'ctx', split_axis=0, concat_axis=0, tiled=True)  109 us
    reduce_scatter x1, waiting for transfers between devices, per_device(): lax.psum_scatter(combined.astype(jnp.bfloat16), 'exp', scatter_dimension=...  38.7 us
    reduce_scatter x1, waiting for transfers between devices, per_device(): lax.psum_scatter(jnp.dot(attended, out_weight, preferred_element_type=jnp...  23.8 us
    scatter x1, local copies, waits for them, and re-layouts, per_device(): outgoing = jnp.zeros((n_experts * capacity, width), jnp.bfloat16).at[slot...  17.9 us
    dot_general x1, matrix products, per_device(): jnp.dot(activated, down_local, preferred_element_type=jnp.float32)  16.5 us
    all_gather x1, blocking collectives, per_device(): all_normed = lax.all_gather(normed, 'exp', axis=0, tiled=True)  11.3 us
    gather x1, local copies, waits for them, and re-layouts, per_device(): picked = flat_back[slot_index].reshape(rows_here, TOP, width)  9.53 us
  transfers between devices with their start and end apart: 5, of which 3 were waited for; matrix products, arithmetic and copies ran while one was open for 1% of the time, Pallas kernels for 0%

commit v1 on v0

--- a/solution.py
+++ b/solution.py
@@ -10,6 +10,30 @@
 WIN = 128
 NEG_FILL = -1e30
 EPSILON = 1e-05
+
+
+def cut_along(shard, dim, devices):
+    lengths = shard.shape
+    blocks = shard.reshape(*lengths[:dim], devices, lengths[dim] // devices, *lengths[dim + 1 :])
+    return jnp.moveaxis(blocks, dim, 0)
+
+
+def laid_out(pieces, dim):
+    lengths = list(pieces.shape[1:])
+    lengths[dim] *= pieces.shape[0]
+    return jnp.moveaxis(pieces, 0, dim).reshape(lengths)
+
+
+def sent_to_each(x, axis, split_dim, concat_dim):
+    size, position = (lax.axis_size(axis), lax.axis_index(axis))
+    blocks = cut_along(x, split_dim, size)
+    filled = blocks
+    for turn in range(1, size):
+        target, source = ((position + turn) % size, (position - turn) % size)
+        sent = lax.dynamic_index_in_dim(blocks, target, 0)
+        partner_block = lax.ppermute(sent, axis, [(i, (i + turn) % size) for i in range(size)])
+        filled = lax.dynamic_update_slice_in_dim(filled, partner_block, source, axis=0)
+    return laid_out(filled, concat_dim)
 
 
 def shifted(array, axis, by):
@@ -96,7 +120,7 @@
     gate_local = gate_weight[0]
     up_local = up_weight[0]
     down_local = down_weight[0]
-    slot_block = lax.all_to_all(outgoing, "ctx", split_axis=0, concat_axis=0, tiled=True)
+    slot_block = sent_to_each(outgoing, "ctx", 0, 0)
     block_shape = slot_block.shape
     flat_rows = slot_block.reshape(-1, block_shape[2])
     gate_val = jnp.dot(flat_rows, gate_local, preferred_element_type=jnp.float32)

time: 445 us -> 462 us (1.038)
  blocking collectives: 150 us -> 11.3 us
  starting transfers between devices: 11.8 us -> 82.1 us
  waiting for transfers between devices: 172 us -> 239 us
  local copies, waits for them, and re-layouts: 45 us -> 60.5 us
    all_to_all x1 -> x0, blocking collectives: 138 us -> none  [per_device(): lax.all_to_all(outgoing, 'ctx', split_axis=0, concat_axis=0, tiled=True)]
    ppermute x0 -> x15, starting transfers between devices: none -> 69 us  [sent_to_each(): lax.ppermute(sent, axis, [(i, (i + turn) % size) for i in range(size)])]
    ppermute x0 -> x15, waiting for transfers between devices: none -> 67.6 us  [sent_to_each(): lax.ppermute(sent, axis, [(i, (i + turn) % size) for i in range(size)])]
    dynamic_update_slice x0 -> x14, local copies, waits for them, and re-layouts: none -> 12.8 us  [sent_to_each(): lax.dynamic_update_slice_in_dim(filled, partner_block, source, axis=0)]
    dynamic_slice x0 -> x2, local copies, waits for them, and re-layouts: none -> 5.25 us  [sent_to_each(): sent = lax.dynamic_index_in_dim(blocks, target, 0)]
  transfers between devices with their start and end apart: 5 -> 20, of which waited for: 3 -> 9; matrix products, arithmetic and copies ran while one was open for 1% -> 4% of each run, Pallas kernels for 0% -> 0%
where the time goes in v1:
time: 462 us; the launch traced here: 457 us
  waiting for transfers between devices  239 us (52%)
  starting transfers between devices  82.1 us (18%)
  local copies, waits for them, and re-layouts  60.5 us (13%)
  matrix products  33.4 us (7%)
  other arithmetic  16.3 us (4%)
  between operations  14.4 us (3%)
  blocking collectives  11.3 us (2%)
    all_to_all x1, waiting for transfers between devices, per_device(): lax.all_to_all(partial_out, 'ctx', split_axis=0, concat_axis=0, tiled=True)  109 us
    ppermute x15, starting transfers between devices, sent_to_each(): lax.ppermute(sent, axis, [(i, (i + turn) % size) for i in range(size)])  69 us
    ppermute x15, waiting for transfers between devices, sent_to_each(): lax.ppermute(sent, axis, [(i, (i + turn) % size) for i in range(size)])  67.6 us
    reduce_scatter x1, waiting for transfers between devices, per_device(): lax.psum_scatter(combined.astype(jnp.bfloat16), 'exp', scatter_dimension=...  38.8 us
    reduce_scatter x1, waiting for transfers between devices, per_device(): lax.psum_scatter(jnp.dot(attended, out_weight, preferred_element_type=jnp...  23.7 us
    scatter x1, local copies, waits for them, and re-layouts, per_device(): outgoing = jnp.zeros((n_experts * capacity, width), jnp.bfloat16).at[slot...  17.9 us
    dot_general x1, matrix products, per_device(): jnp.dot(activated, down_local, preferred_element_type=jnp.float32)  16.5 us
    dynamic_update_slice x14, local copies, waits for them, and re-layouts, sent_to_each(): lax.dynamic_update_slice_in_dim(filled, partner_block, source, axis=0)  12.8 us
  transfers between devices with their start and end apart: 20, of which 9 were waited for; matrix products, arithmetic and copies ran while one was open for 4% of the time, Pallas kernels for 0%

profile of v1, /device:TPU:0, one launch (start us, length us, event | category | flops | bytes accessed | tf_op | source)
XLA Modules:
  0.0 457.5 jit_solution(8786692037535295438)
XLA Ops:
  8.9 4.5 collective-permute-start
  19.3 6.0 %fusion.29 = f32[128,2880]{1,0:T(8,128)} fusion(bf16[128,1024]{0,1:T(8,128)(2,1)S(1)} %bitcast.76, bf16[1024,2880]{0,1:T(8,128)(2,1)} %param.17), kind=kOutput, calls=%fused_computation.94 | convolution fusion | flops 754974720 | bytes 7634944 | tf_op jit(solution)/shard_map/dot_general | solution.py:95
  27.5 23.7 %reduce-scatter.3.cloned.1.call-done = f32[64,2880]{1,0:T(8,128)} async-done(((f32[128,2880]{1,0:T(8,128)}), f32[64,2880]{1,0:T(8,128)}) %reduce-scatter.3.cloned.1.call-update) | async-done | bytes 737296 | tf_op jit(solution)/shard_map/reduce_scatter | solution.py:94
  53.8 11.3 %all_gather.3 = bf16[128,2880]{1,0:T(8,128)(2,1)S(1)} all-gather(bf16[64,2880]{1,0:T(8,128)(2,1)S(1)} %multiply_convert_fusion.2), channel_id=1, replica_groups=mesh['ctx'=16,'exp'=2] {'exp'}, dimensions={0}, use_global_device_ids=true | all-gather | bytes 1105920 | tf_op jit(solution)/shard_map/all_gather | solution.py:103
  65.2 17.9 %scatter_custom_fusion = bf16[1024,2880]{1,0:T(8,128)(2,1)} fusion(s32[512]{0:T(512)S(1)} %bitcast.78, bf16[128,2880]{1,0:T(8,128)(2,1)S(1)} %all_gather.3, s32[1024]{0:T(1024)S(1)} %pad_clamp_fusion.1, bf16[]{:T(256)} %constant.257.clone.1), kind=kCustom, calls=%fused_computation.11 | custom fusion | bytes 5898242 | tf_op jit(solution)/shard_map/scatter | solution.py:117
  84.3 9.6 %collective-permute-done.2 = bf16[1,1,64,2880]{3,2,0,1:T(8,128)(2,1)} collective-permute-done((bf16[1,1,64,2880]{3,2,0,1:T(8,128)(2,1)S(1)}, bf16[1,1,64,2880]{3,2,0,1:T(8,128)(2,1)}, u32[]{:S(2)}, u32[]{:S(2)}) %collective-permute-start.2) | collective-permute-done | bytes 368672 | tf_op jit(solution)/shard_map/ppermute | solution.py:34
  94.0 4.2 constant_dynamic-slice_fusion
  103.8 9.2 %collective-permute-done.3 = bf16[1,1,64,2880]{3,2,0,1:T(8,128)(2,1)} collective-permute-done((bf16[1,1,64,2880]{3,2,0,1:T(8,128)(2,1)}, bf16[1,1,64,2880]{3,2,0,1:T(8,128)(2,1)}, u32[]{:S(2)}, u32[]{:S(2)}) %collective-permute-start.3) | collective-permute-done | bytes 368672 | tf_op jit(solution)/shard_map/ppermute | solution.py:34
  116.5 8.4 %collective-permute-start.10 = (bf16[1,1,64,2880]{3,2,0,1:T(8,128)(2,1)S(1)}, bf16[1,1,64,2880]{3,2,0,1:T(8,128)(2,1)S(1)}, u32[]{:S(2)}, u32[]{:S(2)}) collective-permute-start(bf16[1,1,64,2880]{3,2,0,1:T(8,128)(2,1)S(1)} %get-tuple-element.11), channel_id=1, source_target_pairs={{0,18},{2,20},{4,22},{6,24},{8,26},{10,28},{12,30},{14,0},{16,2},{... | collective-permute-start | bytes 1105928 | tf_op jit(solution)/shard_map/ppermute | solution.py:34
  125.6 42.1 %collective-permute-done.6 = bf16[1,1,64,2880]{3,2,0,1:T(8,128)(2,1)S(1)} collective-permute-done((bf16[1,1,64,2880]{3,2,0,1:T(8,128)(2,1)}, bf16[1,1,64,2880]{3,2,0,1:T(8,128)(2,1)S(1)}, u32[]{:S(2)}, u32[]{:S(2)}) %collective-permute-start.6) | collective-permute-done | bytes 368672 | tf_op jit(solution)/shard_map/ppermute | solution.py:34
  168.7 15.7 %collective-permute-start.12 = (bf16[1,1,64,2880]{3,2,0,1:T(8,128)(2,1)S(1)}, bf16[1,1,64,2880]{3,2,0,1:T(8,128)(2,1)S(1)}, u32[]{:S(2)}, u32[]{:S(2)}) collective-permute-start(bf16[1,1,64,2880]{3,2,0,1:T(8,128)(2,1)S(1)} %get-tuple-element.9), channel_id=1, source_target_pairs={{0,22},{2,24},{4,26},{6,28},{8,30},{10,0},{12,2},{14,4},{16,6},{18... | collective-permute-start | bytes 1105928 | tf_op jit(solution)/shard_map/ppermute | solution.py:34
  185.2 12.8 %collective-permute-start.13 = (bf16[1,1,64,2880]{3,2,0,1:T(8,128)(2,1)S(1)}, bf16[1,1,64,2880]{3,2,0,1:T(8,128)(2,1)S(1)}, u32[]{:S(2)}, u32[]{:S(2)}) collective-permute-start(bf16[1,1,64,2880]{3,2,0,1:T(8,128)(2,1)S(1)} %get-tuple-element.8), channel_id=1, source_target_pairs={{0,24},{2,26},{4,28},{6,30},{8,0},{10,2},{12,4},{14,6},{16,8},{18,... | collective-permute-start | bytes 1105928 | tf_op jit(solution)/shard_map/ppermute | solution.py:34
  198.8 14.8 %collective-permute-start.14 = (bf16[1,1,64,2880]{3,2,0,1:T(8,128)(2,1)S(1)}, bf16[1,1,64,2880]{3,2,0,1:T(8,128)(2,1)S(1)}, u32[]{:S(2)}, u32[]{:S(2)}) collective-permute-start(bf16[1,1,64,2880]{3,2,0,1:T(8,128)(2,1)S(1)} %get-tuple-element.7), channel_id=1, source_target_pairs={{0,26},{2,28},{4,30},{6,0},{8,2},{10,4},{12,6},{14,8},{16,10},{18,... | collective-permute-start | bytes 1105928 | tf_op jit(solution)/shard_map/ppermute | solution.py:34
  214.4 5.0 %collective-permute-start.15 = (bf16[1,1,64,2880]{3,2,0,1:T(8,128)(2,1)S(1)}, bf16[1,1,64,2880]{3,2,0,1:T(8,128)(2,1)S(1)}, u32[]{:S(2)}, u32[]{:S(2)}) collective-permute-start(bf16[1,1,64,2880]{3,2,0,1:T(8,128)(2,1)S(1)} %get-tuple-element.6), channel_id=1, source_target_pairs={{0,28},{2,30},{4,0},{6,2},{8,4},{10,6},{12,8},{14,10},{16,12},{18,... | collective-permute-start | bytes 1105928 | tf_op jit(solution)/shard_map/ppermute | solution.py:34
  220.1 7.0 %collective-permute-start.16 = (bf16[1,1,64,2880]{3,2,0,1:T(8,128)(2,1)S(1)}, bf16[1,1,64,2880]{3,2,0,1:T(8,128)(2,1)S(1)}, u32[]{:S(2)}, u32[]{:S(2)}) collective-permute-start(bf16[1,1,64,2880]{3,2,0,1:T(8,128)(2,1)S(1)} %get-tuple-element.5), channel_id=1, source_target_pairs={{0,30},{2,0},{4,2},{6,4},{8,6},{10,8},{12,10},{14,12},{16,14},{18,... | collective-permute-start | bytes 1105928 | tf_op jit(solution)/shard_map/ppermute | solution.py:34
  231.6 6.0 %collective-permute-done.16 = bf16[1,1,64,2880]{3,2,0,1:T(8,128)(2,1)S(1)} collective-permute-done((bf16[1,1,64,2880]{3,2,0,1:T(8,128)(2,1)S(1)}, bf16[1,1,64,2880]{3,2,0,1:T(8,128)(2,1)S(1)}, u32[]{:S(2)}, u32[]{:S(2)}) %collective-permute-start.16) | collective-permute-done | bytes 368672 | tf_op jit(solution)/shard_map/ppermute | solution.py:34
  238.3 9.7 %fusion.1 = f32[1024,768]{1,0:T(8,128)} fusion(bf16[1024,2880]{1,0:T(8,128)(2,1)} %bitcast.72, bf16[1,2880,768]{2,1,0:T(8,128)(2,1)} %param.20), kind=kOutput, calls=%fused_computation.6 | convolution fusion | flops 4529848320 | bytes 13467648 | tf_op jit(solution)/shard_map/dot_general | solution.py:127
  248.0 16.5 %convolution_convert_fusion = bf16[1024,2880]{0,1:T(8,128)(2,1)} fusion(bf16[1,768,2880]{1,2,0:T(8,128)(2,1)} %param.21, f32[1024,768]{1,0:T(8,128)} %fusion.1, bf16[1024,2880]{1,0:T(8,128)(2,1)} %bitcast.73, bf16[1,2880,768]{2,1,0:T(8,128)(2,1)} %param.19), kind=kOutput, calls=%fused_computation.4 | convolution fusion | flops 9067364352 | bytes 23789568 | tf_op jit(solution)/shard_map/dot_general | solution.py:129
  264.5 8.5 %copy.27 = bf16[1024,2880]{1,0:T(8,128)(2,1)} copy(bf16[1024,2880]{0,1:T(8,128)(2,1)} %convolution_convert_fusion) | data formatting | bytes 11796480 | tf_op jit(solution)/shard_map/convert_element_type | solution.py:129
  273.0 6.1 %all-to-all-start = ((bf16[16,64,2880]{2,1,0:T(8,128)(2,1)}), bf16[16,64,2880]{2,1,0:T(8,128)(2,1)}, u32[]{:S(2)}, u32[]{:S(2)}) async-start(bf16[16,64,2880]{2,1,0:T(8,128)(2,1)} %bitcast.69), calls=%async_computation.1 | async-start | bytes 12058624 | tf_op jit(solution)/shard_map/all_to_all | solution.py:133
  279.4 109.3 %all-to-all-done = bf16[16,64,2880]{2,1,0:T(8,128)(2,1)} async-done(((bf16[16,64,2880]{2,1,0:T(8,128)(2,1)}), bf16[16,64,2880]{2,1,0:T(8,128)(2,1)}, u32[]{:S(2)}, u32[]{:S(2)}) %all-to-all-start) | async-done | bytes 5898272 | tf_op jit(solution)/shard_map/all_to_all | solution.py:133
  388.7 9.5 %gather_fusion = bf16[512,2880]{1,0:T(8,128)(2,1)S(1)} fusion(bf16[1024,2880]{1,0:T(8,128)(2,1)} %bitcast.20, s32[1024]{0:T(1024)S(1)} %pad_clamp_fusion), kind=kCustom, calls=%fused_computation.1 | custom fusion | bytes 5900288 | tf_op jit(solution)/shard_map/gather | solution.py:135
  401.8 8.0 %multiply_reduce_fusion = bf16[128,2880]{1,0:T(8,128)(2,1)} fusion(f32[128,4,2880]{2,1,0:T(4,128)} %reshape.227, f32[128,4]{1,0:T(8,128)S(1)} %copy.28), kind=kLoop, calls=%fused_computation.3 | loop fusion | flops 2580480 | bytes 6637568 | tf_op jit(solution)/shard_map/reduce_sum | solution.py:136
  409.8 38.8 %reduce-scatter.5.cloned.1.call-done = bf16[64,2880]{1,0:T(8,128)(2,1)} async-done(((bf16[128,2880]{1,0:T(8,128)(2,1)}), bf16[64,2880]{1,0:T(8,128)(2,1)}) %reduce-scatter.5.cloned.1.call-update) | async-done | bytes 368656 | tf_op jit(solution)/shard_map/reduce_scatter | solution.py:137
  (90 shorter events, 38.4 us)
Async XLA Ops:
  6.5 44.7 %reduce-scatter.3.cloned.1.call-start = ((), (), s32[]{:S(2)}) async-start(), calls=%async_computation.3 | async-start | bytes 2260992 | tf_op jit(solution)/shard_map/reduce_scatter | solution.py:94
  6.5 9.0 %collective-permute-start.1 = (bf16[128,256]{1,0:T(8,128)(2,1)}, bf16[128,256]{1,0:T(8,128)(2,1)S(1)}, u32[]{:S(2)}, u32[]{:S(2)}) collective-permute-start(bf16[128,256]{1,0:T(8,128)(2,1)} %param.14), channel_id=1, source_target_pairs={{0,2},{2,4},{4,6},{6,8},{8,10},{10,12},{12,14},{14,16},{16,18},{18... | collective-permute-start | bytes 196616 | tf_op jit(solution)/shard_map/ppermute | solution.py:42
  8.9 8.7 %collective-permute-start = (bf16[128,256]{1,0:T(8,128)(2,1)}, bf16[128,256]{1,0:T(8,128)(2,1)S(1)}, u32[]{:S(2)}, u32[]{:S(2)}) collective-permute-start(bf16[128,256]{1,0:T(8,128)(2,1)} %param.15), channel_id=1, source_target_pairs={{0,2},{2,4},{4,6},{6,8},{8,10},{10,12},{12,14},{14,16},{16,18},{18... | collective-permute-start | bytes 196616 | tf_op jit(solution)/shard_map/ppermute | solution.py:42
  19.3 31.9 %copy-start.1 = (bf16[64,2880]{1,0:T(8,128)(2,1)S(1)}, bf16[64,2880]{1,0:T(8,128)(2,1)}, u32[]{:S(2)}) copy-start(bf16[64,2880]{1,0:T(8,128)(2,1)} %param.12) | copy-start | bytes 1105924
  19.3 33.2 %copy-start.2 = (f32[2880]{0:T(1024)S(1)}, f32[2880]{0:T(1024)}, u32[]{:S(2)}) copy-start(f32[2880]{0:T(1024)} %param.18) | copy-start | bytes 34564
  84.1 9.9 %collective-permute-start.2 = (bf16[1,1,64,2880]{3,2,0,1:T(8,128)(2,1)S(1)}, bf16[1,1,64,2880]{3,2,0,1:T(8,128)(2,1)}, u32[]{:S(2)}, u32[]{:S(2)}) collective-permute-start(bf16[1,1,64,2880]{3,2,0,1:T(8,128)(2,1)S(1)} %constant_dynamic-slice_fusion.14), channel_id=1, source_target_pairs={{0,2},{2,4},{4,6},{6,8},{8,10},{10,12},{12,14},{14,16},{16,18},{18... | collective-permute-start | bytes 1105928 | tf_op jit(solution)/shard_map/ppermute | solution.py:34
  98.2 14.7 %collective-permute-start.3 = (bf16[1,1,64,2880]{3,2,0,1:T(8,128)(2,1)}, bf16[1,1,64,2880]{3,2,0,1:T(8,128)(2,1)}, u32[]{:S(2)}, u32[]{:S(2)}) collective-permute-start(bf16[1,1,64,2880]{3,2,0,1:T(8,128)(2,1)} %get-tuple-element.18), channel_id=1, source_target_pairs={{0,4},{2,6},{4,8},{6,10},{8,12},{10,14},{12,16},{14,18},{16,20},{1... | collective-permute-start | bytes 1105928 | tf_op jit(solution)/shard_map/ppermute | solution.py:34
  98.2 16.5 %collective-permute-start.4 = (bf16[1,1,64,2880]{3,2,0,1:T(8,128)(2,1)}, bf16[1,1,64,2880]{3,2,0,1:T(8,128)(2,1)}, u32[]{:S(2)}, u32[]{:S(2)}) collective-permute-start(bf16[1,1,64,2880]{3,2,0,1:T(8,128)(2,1)} %get-tuple-element.17), channel_id=1, source_target_pairs={{0,6},{2,8},{4,10},{6,12},{8,14},{10,16},{12,18},{14,20},{16,22},{... | collective-permute-start | bytes 1105928 | tf_op jit(solution)/shard_map/ppermute | solution.py:34
  98.5 17.9 %collective-permute-start.5 = (bf16[1,1,64,2880]{3,2,0,1:T(8,128)(2,1)}, bf16[1,1,64,2880]{3,2,0,1:T(8,128)(2,1)S(1)}, u32[]{:S(2)}, u32[]{:S(2)}) collective-permute-start(bf16[1,1,64,2880]{3,2,0,1:T(8,128)(2,1)} %get-tuple-element.16), channel_id=1, source_target_pairs={{0,8},{2,10},{4,12},{6,14},{8,16},{10,18},{12,20},{14,22},{16,24},... | collective-permute-start | bytes 1105928 | tf_op jit(solution)/shard_map/ppermute | solution.py:34
  98.6 69.1 %collective-permute-start.6 = (bf16[1,1,64,2880]{3,2,0,1:T(8,128)(2,1)}, bf16[1,1,64,2880]{3,2,0,1:T(8,128)(2,1)S(1)}, u32[]{:S(2)}, u32[]{:S(2)}) collective-permute-start(bf16[1,1,64,2880]{3,2,0,1:T(8,128)(2,1)} %get-tuple-element.15), channel_id=1, source_target_pairs={{0,10},{2,12},{4,14},{6,16},{8,18},{10,20},{12,22},{14,24},{16,26}... | collective-permute-start | bytes 1105928 | tf_op jit(solution)/shard_map/ppermute | solution.py:34
  100.8 67.8 %collective-permute-start.7 = (bf16[1,1,64,2880]{3,2,0,1:T(8,128)(2,1)}, bf16[1,1,64,2880]{3,2,0,1:T(8,128)(2,1)S(1)}, u32[]{:S(2)}, u32[]{:S(2)}) collective-permute-start(bf16[1,1,64,2880]{3,2,0,1:T(8,128)(2,1)} %get-tuple-element.14), channel_id=1, source_target_pairs={{0,12},{2,14},{4,16},{6,18},{8,20},{10,22},{12,24},{14,26},{16,28}... | collective-permute-start | bytes 1105928 | tf_op jit(solution)/shard_map/ppermute | solution.py:34
  112.9 72.3 %collective-permute-start.8 = (bf16[1,1,64,2880]{3,2,0,1:T(8,128)(2,1)}, bf16[1,1,64,2880]{3,2,0,1:T(8,128)(2,1)S(1)}, u32[]{:S(2)}, u32[]{:S(2)}) collective-permute-start(bf16[1,1,64,2880]{3,2,0,1:T(8,128)(2,1)} %get-tuple-element.13), channel_id=1, source_target_pairs={{0,14},{2,16},{4,18},{6,20},{8,22},{10,24},{12,26},{14,28},{16,30}... | collective-permute-start | bytes 1105928 | tf_op jit(solution)/shard_map/ppermute | solution.py:34
  114.7 84.0 %collective-permute-start.9 = (bf16[1,1,64,2880]{3,2,0,1:T(8,128)(2,1)S(1)}, bf16[1,1,64,2880]{3,2,0,1:T(8,128)(2,1)S(1)}, u32[]{:S(2)}, u32[]{:S(2)}) collective-permute-start(bf16[1,1,64,2880]{3,2,0,1:T(8,128)(2,1)S(1)} %get-tuple-element.12), channel_id=1, source_target_pairs={{0,16},{2,18},{4,20},{6,22},{8,24},{10,26},{12,28},{14,30},{16,0},... | collective-permute-start | bytes 1105928 | tf_op jit(solution)/shard_map/ppermute | solution.py:34
  116.5 97.9 %collective-permute-start.10 = (bf16[1,1,64,2880]{3,2,0,1:T(8,128)(2,1)S(1)}, bf16[1,1,64,2880]{3,2,0,1:T(8,128)(2,1)S(1)}, u32[]{:S(2)}, u32[]{:S(2)}) collective-permute-start(bf16[1,1,64,2880]{3,2,0,1:T(8,128)(2,1)S(1)} %get-tuple-element.11), channel_id=1, source_target_pairs={{0,18},{2,20},{4,22},{6,24},{8,26},{10,28},{12,30},{14,0},{16,2},{... | collective-permute-start | bytes 1105928 | tf_op jit(solution)/shard_map/ppermute | solution.py:34
  167.7 52.4 %collective-permute-start.11 = (bf16[1,1,64,2880]{3,2,0,1:T(8,128)(2,1)S(1)}, bf16[1,1,64,2880]{3,2,0,1:T(8,128)(2,1)S(1)}, u32[]{:S(2)}, u32[]{:S(2)}) collective-permute-start(bf16[1,1,64,2880]{3,2,0,1:T(8,128)(2,1)S(1)} %get-tuple-element.10), channel_id=1, source_target_pairs={{0,20},{2,22},{4,24},{6,26},{8,28},{10,30},{12,0},{14,2},{16,4},{1... | collective-permute-start | bytes 1105928 | tf_op jit(solution)/shard_map/ppermute | solution.py:34
  168.7 59.2 %collective-permute-start.12 = (bf16[1,1,64,2880]{3,2,0,1:T(8,128)(2,1)S(1)}, bf16[1,1,64,2880]{3,2,0,1:T(8,128)(2,1)S(1)}, u32[]{:S(2)}, u32[]{:S(2)}) collective-permute-start(bf16[1,1,64,2880]{3,2,0,1:T(8,128)(2,1)S(1)} %get-tuple-element.9), channel_id=1, source_target_pairs={{0,22},{2,24},{4,26},{6,28},{8,30},{10,0},{12,2},{14,4},{16,6},{18... | collective-permute-start | bytes 1105928 | tf_op jit(solution)/shard_map/ppermute | solution.py:34
  185.2 43.5 %collective-permute-start.13 = (bf16[1,1,64,2880]{3,2,0,1:T(8,128)(2,1)S(1)}, bf16[1,1,64,2880]{3,2,0,1:T(8,128)(2,1)S(1)}, u32[]{:S(2)}, u32[]{:S(2)}) collective-permute-start(bf16[1,1,64,2880]{3,2,0,1:T(8,128)(2,1)S(1)} %get-tuple-element.8), channel_id=1, source_target_pairs={{0,24},{2,26},{4,28},{6,30},{8,0},{10,2},{12,4},{14,6},{16,8},{18,... | collective-permute-start | bytes 1105928 | tf_op jit(solution)/shard_map/ppermute | solution.py:34
  198.8 30.7 %collective-permute-start.14 = (bf16[1,1,64,2880]{3,2,0,1:T(8,128)(2,1)S(1)}, bf16[1,1,64,2880]{3,2,0,1:T(8,128)(2,1)S(1)}, u32[]{:S(2)}, u32[]{:S(2)}) collective-permute-start(bf16[1,1,64,2880]{3,2,0,1:T(8,128)(2,1)S(1)} %get-tuple-element.7), channel_id=1, source_target_pairs={{0,26},{2,28},{4,30},{6,0},{8,2},{10,4},{12,6},{14,8},{16,10},{18,... | collective-permute-start | bytes 1105928 | tf_op jit(solution)/shard_map/ppermute | solution.py:34
  214.4 16.4 %collective-permute-start.15 = (bf16[1,1,64,2880]{3,2,0,1:T(8,128)(2,1)S(1)}, bf16[1,1,64,2880]{3,2,0,1:T(8,128)(2,1)S(1)}, u32[]{:S(2)}, u32[]{:S(2)}) collective-permute-start(bf16[1,1,64,2880]{3,2,0,1:T(8,128)(2,1)S(1)} %get-tuple-element.6), channel_id=1, source_target_pairs={{0,28},{2,30},{4,0},{6,2},{8,4},{10,6},{12,8},{14,10},{16,12},{18,... | collective-permute-start | bytes 1105928 | tf_op jit(solution)/shard_map/ppermute | solution.py:34
  220.1 17.4 %collective-permute-start.16 = (bf16[1,1,64,2880]{3,2,0,1:T(8,128)(2,1)S(1)}, bf16[1,1,64,2880]{3,2,0,1:T(8,128)(2,1)S(1)}, u32[]{:S(2)}, u32[]{:S(2)}) collective-permute-start(bf16[1,1,64,2880]{3,2,0,1:T(8,128)(2,1)S(1)} %get-tuple-element.5), channel_id=1, source_target_pairs={{0,30},{2,0},{4,2},{6,4},{8,6},{10,8},{12,10},{14,12},{16,14},{18,... | collective-permute-start | bytes 1105928 | tf_op jit(solution)/shard_map/ppermute | solution.py:34
  273.0 6.2 %copy-start.4 = (f32[128,4]{0,1:T(4,128)S(1)}, f32[128,4]{0,1:T(4,128)}, u32[]{:S(2)}) copy-start(f32[128,4]{0,1:T(4,128)} %param.23) | copy-start | bytes 6148
  273.0 115.7 %all-to-all-start = ((bf16[16,64,2880]{2,1,0:T(8,128)(2,1)}), bf16[16,64,2880]{2,1,0:T(8,128)(2,1)}, u32[]{:S(2)}, u32[]{:S(2)}) async-start(bf16[16,64,2880]{2,1,0:T(8,128)(2,1)} %bitcast.69), calls=%async_computation.1 | async-start | bytes 12058624 | tf_op jit(solution)/shard_map/all_to_all | solution.py:133
  279.2 169.4 %reduce-scatter.5.cloned.1.call-start = ((), (), s32[]{:S(2)}) async-start(), calls=%async_computation.4 | async-start | bytes 1130496 | tf_op jit(solution)/shard_map/reduce_scatter | solution.py:137
  401.8 46.8 %copy-start = (f32[64,2880]{1,0:T(8,128)S(1)}, f32[64,2880]{1,0:T(8,128)}, u32[]{:S(2)}) copy-start(f32[64,2880]{1,0:T(8,128)} %reduce-scatter.3.cloned.1.call-done) | copy-start | bytes 2211844
  (1 other events, 6.0 us)
Sparse Core Ops, SparseCore 0:
  25.4 25.7 reduce-scatter.2
  409.9 38.5 reduce-scatter.4
